TPU v7x, 256 devices: a whole 4x4x8 slice. The times are simulated.
256 devices in a mesh: rep: 4 (over y), fsdp: 64 (over x, z, core).
Axes of the slice: x: 4, y: 4, z: 8, core: 2. Of those that a mesh axis runs over, the one named last changes fastest.
Arguments:
- activations: bfloat16 [65536, 512], P(('rep', 'fsdp')), may hold values from -6 to 6
- output_grads: bfloat16 [65536, 8192], P(('rep', 'fsdp'))
- master: float32 [8192, 512], P('fsdp'), may hold values from -6 to 6
- first_moment: float32 [8192, 512], P('fsdp'), may hold values from -4 to 4
- second_moment: float32 [8192, 512], P('fsdp'), may hold values from 0.2 to 2
Outputs:
- new_master: float32 [8192, 512], P('fsdp')
- new_first: float32 [8192, 512], P('fsdp')
- new_second: float32 [8192, 512], P('fsdp')
- params: bfloat16 [8192, 512], replicated
All inputs are finite; a program needn't handle non-finite values.
Results may differ from a plain program's by a relative error of at most 0.0004.
Values may be sent and summed in bfloat16 or wider, within the bound.
No kernel may reach another device: no remote copies, remote signals or barrier semaphores. Data moves between devices by JAX's collectives and lax.ppermute only.
A program may use at most 128 MiB of HBM per device.

v0:
```python
import jax
import jax.numpy as jnp
from jax import lax
from jax.sharding import PartitionSpec as P

dot_epsilon = 1e-06
beta_one = 0.9
beta_two = 0.95
adam_epsilon = 1e-08
learn_rate = 0.02
decay_rate = 0.1
contract_first = (((0,), (0,)), ((), ()))


def swapped(shard, axis, apart):
    return lax.ppermute(shard, axis, [(i, i ^ 1 << apart) for i in range(lax.axis_size(axis))])


def reversed_bits(number_in, bit_count):
    result = 0
    for position in range(bit_count):
        result = result << 1 | number_in >> position & 1
    return result


def local(activations, output_grads, master, first_moment, second_moment):
    grad_shard = lax.psum_scatter(
        lax.dot_general(
            output_grads, activations, contract_first, preferred_element_type=jnp.float32
        ),
        "fsdp",
        scatter_dimension=0,
        tiled=True,
    )
    replica_count = lax.axis_size("rep")
    level_total = replica_count.bit_length() - 1
    replica = lax.axis_index("rep")
    current = grad_shard
    for level_index in range(level_total):
        side_bit = replica >> level_index & 1
        low_side = side_bit == 0
        half_rows = current.shape[0] // 2
        lower_half = current[:half_rows]
        upper_half = current[half_rows:]
        kept_rows = jnp.where(low_side, lower_half, upper_half)
        outgoing = jnp.where(low_side, upper_half, lower_half)
        incoming = swapped(outgoing, "rep", level_index)
        left_vec = jnp.where(low_side, kept_rows, incoming)
        right_vec = jnp.where(low_side, incoming, kept_rows)
        partial_dots = jnp.stack(
            [
                jnp.sum(left_vec * right_vec),
                jnp.sum(left_vec * left_vec),
                jnp.sum(right_vec * right_vec),
            ]
        )
        totals = lax.psum(partial_dots, "fsdp")
        for inner_bit in range(level_index + 1):
            totals = totals + swapped(totals, "rep", inner_bit)
        left_coef = 1.0 - totals[0] / (2.0 * (totals[1] + dot_epsilon))
        right_coef = 1.0 - totals[0] / (2.0 * (totals[2] + dot_epsilon))
        current = left_coef * left_vec + right_coef * right_vec
    piece_rows = current.shape[0]
    gathered = lax.all_gather(current, "rep", axis=0, tiled=True)
    ordered = [
        gathered[
            reversed_bits(place, level_total)
            * piece_rows : (reversed_bits(place, level_total) + 1)
            * piece_rows
        ]
        for place in range(replica_count)
    ]
    combined = jnp.concatenate(ordered, axis=0)
    correct_one = 1.0 - (beta_one**50) ** 2
    correct_two = 1.0 - (beta_two**50) ** 2
    new_first = beta_one * first_moment + (1.0 - beta_one) * combined
    new_second = beta_two * second_moment + (1.0 - beta_two) * combined * combined
    update = (
        new_first / correct_one / (jnp.sqrt(new_second / correct_two) + adam_epsilon)
        + decay_rate * master
    )
    new_master = master - learn_rate * update
    params = lax.all_gather(new_master.astype(jnp.bfloat16), "fsdp", axis=0, tiled=True)
    return (new_master, new_first, new_second, params)


def solution(mesh):
    in_specs = (
        P(("rep", "fsdp"), None),
        P(("rep", "fsdp"), None),
        P("fsdp", None),
        P("fsdp", None),
        P("fsdp", None),
    )
    out_specs = (P("fsdp", None), P("fsdp", None), P("fsdp", None), P())
    return jax.shard_map(local, mesh=mesh, in_specs=in_specs, out_specs=out_specs, check_vma=False)
```

profile of v0, /device:TPU:1, one launch (start us, length us, event | category | flops | bytes accessed | tf_op | source)
XLA Modules:
  0.0 601.0 jit_solution(10944400333961210456)
XLA Ops:
  7.2 0.9 copy-done
  8.1 10.3 %fusion.6 = f32[8192,512]{1,0:T(8,128)} fusion(bf16[256,8192]{1,0:T(8,128)(2,1)} %param.6, bf16[256,512]{1,0:T(8,128)(2,1)S(1)} %copy-done), kind=kOutput, calls=%fused_computation.27 | convolution fusion | flops 2147483648 | bytes 21233664 | tf_op jit(solution)/shard_map/dot_general | solution.py:28
  18.5 189.2 %reduce-scatter.2.cloned.1.call-done = f32[128,512]{1,0:T(8,128)} async-done(((f32[8192,512]{1,0:T(8,128)}), f32[128,512]{1,0:T(8,128)}) %reduce-scatter.2.cloned.1.call-update) | async-done | bytes 262160 | tf_op jit(solution)/shard_map/reduce_scatter | solution.py:27
  207.7 1.0 slice_select_fusion
  208.7 0.9 collective-permute-start
  209.6 3.0 collective-permute-done
  212.6 1.6 multiply_reduce_fusion.2
  214.2 2.0 pad_maximum_fusion.1
  216.2 129.1 %psum.14 = f32[3]{0:T(128)S(1)} all-reduce(f32[3]{0:T(128)S(1)} %pad_maximum_fusion.1), channel_id=1, replica_groups=mesh['rep'=4,'fsdp'=64] {'fsdp'}, use_global_device_ids=true, to_apply=%region_4.5 | all-reduce | flops 3 | bytes 24 | tf_op jit(solution)/shard_map/psum | solution.py:57
  345.3 1.3 collective-permute-start.1
  346.6 1.2 collective-permute-done.1
  351.0 2.6 collective-permute-start.2
  353.7 2.1 collective-permute-done.2
  355.7 0.6 multiply_reduce_fusion.5
  356.4 2.0 pad_maximum_fusion.2
  358.4 126.3 %psum.15 = f32[3]{0:T(128)S(1)} all-reduce(f32[3]{0:T(128)S(1)} %pad_maximum_fusion.2), channel_id=1, replica_groups=mesh['rep'=4,'fsdp'=64] {'fsdp'}, use_global_device_ids=true, to_apply=%region_8.9 | all-reduce | flops 3 | bytes 24 | tf_op jit(solution)/shard_map/psum | solution.py:57
  484.7 1.3 collective-permute-start.3
  486.0 1.2 collective-permute-done.3
  487.2 2.5 collective-permute-start.4
  489.7 1.3 collective-permute-done.4
  494.3 9.5 %all_gather.6 = f32[128,512]{1,0:T(8,128)S(1)} all-gather(f32[32,512]{1,0:T(8,128)S(1)} %multiply_add_fusion.2), channel_id=1, replica_groups=mesh['rep'=4,'fsdp'=64] {'rep'}, dimensions={0}, use_global_device_ids=true | all-gather | bytes 327680 | tf_op jit(solution)/shard_map/all_gather | solution.py:64
  503.9 1.1 fusion.1
  504.9 81.9 %all-gather.2.cloned.1.call-done = bf16[8192,512]{1,0:T(8,128)(2,1)} async-done(((bf16[128,512]{1,0:T(8,128)(2,1)}), bf16[8192,512]{1,0:T(8,128)(2,1)}) %all-gather.2.cloned.1.call-update) | async-done | bytes 8388624 | tf_op jit(solution)/shard_map/all_gather | solution.py:83
  586.9 7.3 %copy.10 = bf16[8192,512]{1,0:T(8,128)(2,1)} copy(bf16[8192,512]{1,0:T(8,128)(2,1)} %all-gather.2.cloned.1.call-done) | data formatting | bytes 16777216
  (20 shorter events, 1.4 us)
Async XLA Ops:
  7.2 1.0 copy-start
  7.2 200.5 %reduce-scatter.2.cloned.1.call-start = ((), (), s32[]{:S(2)}) async-start(), calls=%async_computation.1 | async-start | bytes 17039360 | tf_op jit(solution)/shard_map/reduce_scatter | solution.py:27
  18.4 485.4 %copy-start.1 = (f32[128,512]{1,0:T(8,128)S(1)}, f32[128,512]{1,0:T(8,128)}, u32[]{:S(2)}) copy-start(f32[128,512]{1,0:T(8,128)} %param.7) | copy-start | bytes 786436
  18.4 485.4 %copy-start.2 = (f32[128,512]{1,0:T(8,128)S(1)}, f32[128,512]{1,0:T(8,128)}, u32[]{:S(2)}) copy-start(f32[128,512]{1,0:T(8,128)} %param.8) | copy-start | bytes 786436
  18.4 485.5 %copy-start.3 = (f32[128,512]{1,0:T(8,128)S(1)}, f32[128,512]{1,0:T(8,128)}, u32[]{:S(2)}) copy-start(f32[128,512]{1,0:T(8,128)} %param.9) | copy-start | bytes 786436
  18.4 568.4 %all-gather.2.cloned.1.call-start = ((), (), s32[]{:S(2)}) async-start(), calls=%async_computation.2 | async-start | bytes 8519680 | tf_op jit(solution)/shard_map/all_gather | solution.py:83
  208.7 3.9 collective-permute-start
  345.3 2.5 collective-permute-start.1
  351.0 4.7 collective-permute-start.2
  484.7 2.5 collective-permute-start.3
  487.2 3.9 collective-permute-start.4
Sparse Core Ops, SparseCore 0:
  18.6 189.1 reduce-scatter.1
  505.1 81.7 all-gather.1
where the time goes:
time: 601 us
  waiting for transfers between devices  280 us (47%)
  blocking collectives  265 us (44%)
  between operations  19.3 us (3%)
  matrix products  10.3 us (2%)
  local copies, waits for them, and re-layouts  9.44 us (2%)
  starting transfers between devices  8.68 us (1%)
  other arithmetic  8.38 us (1%)
    psum x2, blocking collectives, local(): totals = lax.psum(partial_dots, 'fsdp')  255 us
    reduce_scatter x1, waiting for transfers between devices, local(): lax.psum_scatter(lax.dot_general(output_grads, activations, contract_firs...  189 us
    all_gather x1, waiting for transfers between devices, local(): lax.all_gather(new_master.astype(jnp.bfloat16), 'fsdp', axis=0, tiled=True)  81.9 us
  transfers between devices with their start and end apart: 7, of which 7 were waited for; matrix products, arithmetic and copies ran while one was open for 0% of the time, Pallas kernels for 0%

commit v1 on v0

--- a/solution.py
+++ b/solution.py
@@ -80,7 +80,12 @@
         + decay_rate * master
     )
     new_master = master - learn_rate * update
-    params = lax.all_gather(new_master.astype(jnp.bfloat16), "fsdp", axis=0, tiled=True)
+    params = jnp.concatenate(
+        lax.all_to_all(
+            jnp.stack([new_master.astype(jnp.bfloat16)] * lax.axis_size("fsdp")), "fsdp", 0, 0
+        ),
+        axis=0,
+    )
     return (new_master, new_first, new_second, params)
 
 

time: 601 us -> 717 us (1.19)
  blocking collectives: 265 us -> 461 us
  waiting for transfers between devices: 280 us -> 198 us
    all_to_all x0 -> x1, blocking collectives: none -> 196 us  [local(): lax.all_to_all(jnp.stack([new_master.astype(jnp.bfloat16)] * lax.axis_siz...]
    all_gather x1 -> x0, waiting for transfers between devices: 81.9 us -> none  [local(): lax.all_gather(new_master.astype(jnp.bfloat16), 'fsdp', axis=0, tiled=True)]
  transfers between devices with their start and end apart: 7 -> 6, of which waited for: 7 -> 6; matrix products, arithmetic and copies ran while one was open for 0% -> 0% of each run, Pallas kernels for 0% -> 0%
where the time goes in v1:
time: 717 us; the launch traced here: 716 us
  blocking collectives  461 us (64%)
  waiting for transfers between devices  198 us (28%)
  between operations  19.3 us (3%)
  local copies, waits for them, and re-layouts  10.4 us (1%)
  matrix products  10.3 us (1%)
  starting transfers between devices  8.64 us (1%)
  other arithmetic  8.34 us (1%)
    psum x2, blocking collectives, local(): totals = lax.psum(partial_dots, 'fsdp')  255 us
    all_to_all x1, blocking collectives, local(): lax.all_to_all(jnp.stack([new_master.astype(jnp.bfloat16)] * lax.axis_siz...  196 us
    reduce_scatter x1, waiting for transfers between devices, local(): lax.psum_scatter(lax.dot_general(output_grads, activations, contract_firs...  189 us
  transfers between devices with their start and end apart: 6, of which 6 were waited for; matrix products, arithmetic and copies ran while one was open for 0% of the time, Pallas kernels for 0%

profile of v1, /device:TPU:1, one launch (start us, length us, event | category | flops | bytes accessed | tf_op | source)
XLA Modules:
  0.0 716.2 jit_solution(7639712770253166810)
XLA Ops:
  7.2 0.9 copy-done
  8.1 10.3 %fusion.6 = f32[8192,512]{1,0:T(8,128)} fusion(bf16[256,8192]{1,0:T(8,128)(2,1)} %param.6, bf16[256,512]{1,0:T(8,128)(2,1)S(1)} %copy-done), kind=kOutput, calls=%fused_computation.27 | convolution fusion | flops 2147483648 | bytes 21233664 | tf_op jit(solution)/shard_map/dot_general | solution.py:28
  18.4 189.3 %reduce-scatter.2.cloned.1.call-done = f32[128,512]{1,0:T(8,128)} async-done(((f32[8192,512]{1,0:T(8,128)}), f32[128,512]{1,0:T(8,128)}) %reduce-scatter.2.cloned.1.call-update) | async-done | bytes 262160 | tf_op jit(solution)/shard_map/reduce_scatter | solution.py:27
  207.7 1.0 slice_select_fusion
  208.7 0.9 collective-permute-start
  209.6 3.0 collective-permute-done
  212.6 1.6 multiply_reduce_fusion.2
  214.2 2.0 pad_maximum_fusion.1
  216.2 129.1 %psum.14 = f32[3]{0:T(128)S(1)} all-reduce(f32[3]{0:T(128)S(1)} %pad_maximum_fusion.1), channel_id=1, replica_groups=mesh['rep'=4,'fsdp'=64] {'fsdp'}, use_global_device_ids=true, to_apply=%region_4.5 | all-reduce | flops 3 | bytes 24 | tf_op jit(solution)/shard_map/psum | solution.py:57
  345.3 1.3 collective-permute-start.1
  346.6 1.2 collective-permute-done.1
  351.0 2.6 collective-permute-start.2
  353.7 2.1 collective-permute-done.2
  356.4 2.0 pad_maximum_fusion.2
  358.4 126.3 %psum.15 = f32[3]{0:T(128)S(1)} all-reduce(f32[3]{0:T(128)S(1)} %pad_maximum_fusion.2), channel_id=1, replica_groups=mesh['rep'=4,'fsdp'=64] {'fsdp'}, use_global_device_ids=true, to_apply=%region_8.9 | all-reduce | flops 3 | bytes 24 | tf_op jit(solution)/shard_map/psum | solution.py:57
  484.7 1.3 collective-permute-start.3
  486.0 1.2 collective-permute-done.3
  487.2 2.5 collective-permute-start.4
  489.7 1.3 collective-permute-done.4
  494.3 9.5 %all_gather.3 = f32[128,512]{1,0:T(8,128)S(1)} all-gather(f32[32,512]{1,0:T(8,128)S(1)} %multiply_add_fusion.2), channel_id=1, replica_groups=mesh['rep'=4,'fsdp'=64] {'rep'}, dimensions={0}, use_global_device_ids=true | all-gather | bytes 327680 | tf_op jit(solution)/shard_map/all_gather | solution.py:64
  503.9 1.0 fusion.1
  504.9 1.0 stack.26
  505.9 196.2 %all_to_all.5 = bf16[64,128,512]{2,1,0:T(8,128)(2,1)} all-to-all(bf16[64,128,512]{2,1,0:T(8,128)(2,1)S(1)} %stack.26), channel_id=1, replica_groups=mesh['rep'=4,'fsdp'=64] {'fsdp'}, dimensions={0} | all-to-all | bytes 16777216 | tf_op jit(solution)/shard_map/all_to_all | solution.py:84
  702.1 7.3 %copy.10 = bf16[8192,512]{1,0:T(8,128)(2,1)} copy(bf16[8192,512]{1,0:T(8,128)(2,1)} %bitcast.13) | data formatting | bytes 16777216
  (19 shorter events, 2.0 us)
Async XLA Ops:
  7.2 1.0 copy-start
  7.2 200.5 %reduce-scatter.2.cloned.1.call-start = ((), (), s32[]{:S(2)}) async-start(), calls=%async_computation.2 | async-start | bytes 17039360 | tf_op jit(solution)/shard_map/reduce_scatter | solution.py:27
  18.4 485.4 %copy-start.1 = (f32[128,512]{1,0:T(8,128)S(1)}, f32[128,512]{1,0:T(8,128)}, u32[]{:S(2)}) copy-start(f32[128,512]{1,0:T(8,128)} %param.7) | copy-start | bytes 786436
  18.4 485.4 %copy-start.2 = (f32[128,512]{1,0:T(8,128)S(1)}, f32[128,512]{1,0:T(8,128)}, u32[]{:S(2)}) copy-start(f32[128,512]{1,0:T(8,128)} %param.8) | copy-start | bytes 786436
  18.4 485.5 %copy-start.3 = (f32[128,512]{1,0:T(8,128)S(1)}, f32[128,512]{1,0:T(8,128)}, u32[]{:S(2)}) copy-start(f32[128,512]{1,0:T(8,128)} %param.9) | copy-start | bytes 786436
  208.7 3.9 collective-permute-start
  345.3 2.5 collective-permute-start.1
  351.0 4.7 collective-permute-start.2
  484.7 2.5 collective-permute-start.3
  487.2 3.9 collective-permute-start.4
Sparse Core Ops, SparseCore 0:
  18.6 189.1 reduce-scatter.1
